TPU v7x, 256 devices: a whole 4x4x8 slice. The times are simulated.
256 devices in a mesh: section: 16 (over y, x_lo, core), ep: 16 (over z, x_hi).
Axes of the slice: x: 4 (x_hi: 2, x_lo: 2; x = x_hi * 2 + x_lo), y: 4, z: 8, core: 2. Of those that a mesh axis runs over, the one named last changes fastest.
Arguments:
- grad_out: bfloat16 [16, 8192, 2048], P('section', 'ep'), may hold values from -0.125 to 0.125
- router_weights: bfloat16 [16, 8192, 8], P('section', 'ep'), may hold values from 0.049804688 to 0.29882812
- expert_ids: int32 [16, 8192, 8], P('section', 'ep'), may hold values from 0 to 127, all different within a row; in each aligned block of 512 rows (0 to 511, 512 to 1023, ..., all dimensions but the last counted through in order) at most 64 rows name the same one
- hidden: bfloat16 [16, 16, 768, 1024], P('section', 'ep'), may hold values from -6 to 6
- master: float32 [16, 16, 768, 1024], P('section', 'ep'), may hold values from -0.25 to 0.25
- moment: bfloat16 [16, 16, 768, 1024], P('section', 'ep'), may hold values from -0.049804688 to 0.049804688
- second: bfloat16 [16, 16, 768, 1024], P('section', 'ep'), may hold values from 0.0019989014 to 0.019897461
Outputs:
- update: float32 [16, 16, 768, 1024], P('section', 'ep')
- router_grad: float32 [16, 8192, 8], P('section', 'ep')
Inputs may be any that keep to these rules, and one draw needn't show every extreme that they name: `expert_ids`: in the rows of one device (aligned blocks of 512 rows) no expert is named by more than 64 rows, a bound that some block reaches.
All inputs are finite; a program needn't handle non-finite values.
Results may differ from a plain program's by a relative error of at most 0.0029.
Values may be sent and summed in bfloat16 or wider, within the bound.
A program may use at most 128 MiB of HBM per device.

v0:
```python
import jax
import jax.numpy as jnp
from jax import lax
from jax.sharding import PartitionSpec as P

beta_first = 0.9
beta_second = 0.95
adam_eps = 1e-08
decay_rate = 0.1
first_fix = 1.0 - 0.9**10
second_fix = 1.0 - 0.95**10


def swapped(array, axis, distance):
    return lax.ppermute(array, axis, [(i, i ^ 1 << distance) for i in range(lax.axis_size(axis))])


def slot_ranks(routes, count):
    onehot = (routes[:, :, None] == jnp.arange(count, dtype=jnp.int32)[None, None, :]).astype(
        jnp.int32
    )
    per_token = jnp.sum(onehot, axis=1)
    before = jnp.cumsum(per_token, axis=0, dtype=jnp.int32) - per_token
    return jnp.sum(before[:, None, :] * onehot, axis=2)


def adam_update(total, param, first, second_moment):
    first_new = beta_first * first + (1.0 - beta_first) * total
    second_new = beta_second * second_moment + (1.0 - beta_second) * total * total
    return (
        first_new / first_fix / (jnp.sqrt(second_new / second_fix) + adam_eps) + decay_rate * param
    )


def scale_hidden(hid_block, slot_weights):
    return (hid_block.astype(jnp.float32) * slot_weights[None, :].astype(jnp.float32)).astype(
        jnp.bfloat16
    )


def project_score(row_block, weight, hid_block):
    proj = jnp.einsum("rd,hd->hr", row_block, weight, preferred_element_type=jnp.float32)
    return jnp.sum(hid_block.astype(jnp.float32) * proj, axis=0)


def local(grad_out, router_weights, expert_ids, hidden, master, moment, second):
    group = lax.axis_size("ep")
    tok_count = grad_out.shape[1]
    top_count = expert_ids.shape[2]
    width = grad_out.shape[2]
    slot_count = hidden.shape[3]
    capacity = slot_count // group
    token_grads = grad_out[0]
    token_weights = router_weights[0]
    routes = expert_ids[0]
    in_flight = routes < group
    slots = slot_ranks(routes, group)
    flat = jnp.where(in_flight, routes * capacity + slots, slot_count).reshape(-1)
    token_index = (
        jnp.arange(tok_count, dtype=jnp.int32)[:, None] + jnp.zeros_like(routes)
    ).reshape(-1)
    inverse = jnp.zeros((slot_count,), jnp.int32).at[flat].set(token_index, mode="drop")
    live = jnp.zeros((slot_count,), jnp.bool_).at[flat].set(True, mode="drop")
    slot_weight = (
        jnp.zeros((slot_count,), jnp.bfloat16).at[flat].set(token_weights.reshape(-1), mode="drop")
    )
    picked = jnp.where(
        live[:, None], jnp.take(token_grads, inverse, axis=0), jnp.zeros((), jnp.bfloat16)
    )
    picked = picked.reshape(group, capacity, width)
    received, received_weight = (
        lax.all_to_all(picked, "ep", split_axis=0, concat_axis=0, tiled=True),
        lax.all_to_all(
            slot_weight.reshape(group, capacity), "ep", split_axis=0, concat_axis=0, tiled=True
        ),
    )
    rows = received.reshape(slot_count, width)
    row_weights = received_weight.reshape(slot_count)
    hid_local = hidden[0, 0]
    param = master[0, 0]
    own_bf = param.astype(jnp.bfloat16)
    half = param.shape[1]
    lower = lax.axis_index("section") < lax.axis_size("section") // 2
    top_bit = lax.axis_size("section").bit_length() - 2
    partner_bf = swapped(own_bf, "section", top_bit)
    full_weights = jnp.where(
        lower, jnp.concatenate([own_bf, partner_bf], 1), jnp.concatenate([partner_bf, own_bf], 1)
    )
    score = project_score(rows, full_weights, hid_local)
    scaled = scale_hidden(hid_local, row_weights)
    grad = jnp.dot(scaled, rows, preferred_element_type=jnp.float32)
    own_grad = jnp.where(lower, grad[:, :half], grad[:, half:])
    outgoing = jnp.where(lower, grad[:, half:], grad[:, :half])
    incoming = swapped(outgoing, "section", top_bit)
    total = own_grad + incoming
    back = lax.all_to_all(
        score.reshape(group, capacity), "ep", split_axis=0, concat_axis=0, tiled=True
    )
    chosen = back.reshape(-1)[jnp.minimum(flat, slot_count - 1)]
    router = jnp.where(in_flight.reshape(-1), chosen, jnp.zeros_like(chosen)).reshape(
        tok_count, top_count
    )
    update = adam_update(
        total, param, moment[0, 0].astype(jnp.float32), second[0, 0].astype(jnp.float32)
    )
    return (update[None, None], router[None])


def solution(mesh):
    placed = (
        P("section", "ep", None),
        P("section", "ep", None),
        P("section", "ep", None),
        P("section", "ep", None, None),
        P("section", "ep", None, None),
        P("section", "ep", None, None),
        P("section", "ep", None, None),
    )
    return jax.shard_map(
        local,
        mesh=mesh,
        in_specs=placed,
        out_specs=(P("section", "ep", None, None), P("section", "ep", None)),
        check_vma=False,
    )
```

profile of v0, /device:TPU:8, one launch (start us, length us, event | category | flops | bytes accessed | tf_op | source)
XLA Modules:
  0.0 359.6 jit_solution(17130230769524094549)
XLA Ops:
  0.6 0.0 copy-start
  0.6 0.9 broadcast_multiply_fusion
  1.5 0.8 copy.27
  2.4 0.8 convert_reduce_fusion
  3.1 1.2 reduce-window.6
  4.3 0.2 slice_reduce_fusion
  4.5 0.1 fusion.22
  4.6 0.8 select_reduce_fusion
  5.4 0.9 copy.32
  6.3 0.2 reshape.181
  6.4 0.1 copy.31
  6.6 0.2 reduce_sum.31
  6.7 0.1 copy.28
  6.9 0.2 mul.82
  7.1 0.2 lt.57
  7.3 0.1 compare_select_fusion
  7.3 28.5 %scatter_custom_fusion = bf16[1024]{0:T(1024)(128)(2,1)S(1)} fusion(s32[4096]{0:T(1024)S(1)} %bitcast.62, bf16[4096]{0:T(1024)(128)(2,1)S(1)} %reshape.181, bf16[]{:T(256)} %constant.26.clone.1), kind=kCustom, calls=%fused_computation.57 | custom fusion | bytes 2050 | tf_op jit(solution)/shard_map/scatter | solution.py:65
  35.9 0.7 all_to_all.20
  36.6 11.0 %all-to-all-start = ((bf16[16,1,64]{2,1,0:T(2,128)(2,1)}), bf16[16,1,64]{2,1,0:T(2,128)(2,1)S(1)}, u32[]{:S(2)}, u32[]{:S(2)}) async-start(bf16[16,1,64]{2,1,0:T(2,128)(2,1)} %all_to_all.20), calls=%async_computation | async-start | bytes 16384 | tf_op jit(solution)/shard_map/all_to_all | solution.py:73
  47.6 0.1 reshape.197
  47.8 15.5 %scatter_custom_fusion.2 = s32[1024]{0:T(1024)S(1)} fusion(s32[4096]{0:T(1024)S(1)} %bitcast.63, s32[4096]{0:T(1024)S(1)} %reshape.197, s32[]{:T(128)} %constant.29.clone.1), kind=kCustom, calls=%fused_computation.53 | custom fusion | bytes 4100 | tf_op jit(solution)/shard_map/scatter | solution.py:62
  63.4 17.6 %scatter_custom_fusion.1 = pred[1024]{0:T(1024)(128)(4,1)S(1)} fusion(s32[4096]{0:T(1024)S(1)} %bitcast.64, pred[4096]{0:T(1024)(128)(4,1)S(1)} %broadcast.120, pred[]{:T(512)} %constant.14.clone.1), kind=kCustom, calls=%fused_computation.55 | custom fusion | bytes 1025 | tf_op jit(solution)/shard_map/scatter | solution.py:63
  81.0 0.1 broadcast_in_dim.62
  81.0 0.1 broadcast_in_dim.65
  81.1 0.0 copy-done
  81.1 6.0 %gather_fusion = bf16[1024,2048]{1,0:T(8,128)(2,1)} fusion(bf16[512,2048]{1,0:T(8,128)(2,1)S(1)} %bitcast.57, s32[1024]{0:T(1024)S(1)} %fusion.23), kind=kCustom, calls=%fused_computation | custom fusion | bytes 8392704 | tf_op jit(solution)/shard_map/jit(_take)/gather | solution.py:68
  87.1 3.8 %select_select_fusion = bf16[16,64,2048]{2,1,0:T(8,128)(2,1)} fusion(bf16[16,64,2048]{2,1,0:T(8,128)(2,1)} %bitcast.58, pred[16,64]{1,0:T(8,128)(4,1)S(1)} %broadcast_in_dim.65, pred[16,64]{1,0:T(8,128)(4,1)S(1)} %broadcast_in_dim.62), kind=kLoop, calls=%fused_computation.6 | loop fusion | flops 4194304 | bytes 8390656 | tf_op jit(solution)/shard_map/jit(_where)/select_n | solution.py:67
  91.0 0.0 all-to-all-done
  91.0 9.7 %all-to-all-start.1 = ((bf16[16,64,2048]{2,1,0:T(8,128)(2,1)}), bf16[16,64,2048]{2,1,0:T(8,128)(2,1)}, u32[]{:S(2)}, u32[]{:S(2)}) async-start(bf16[16,64,2048]{2,1,0:T(8,128)(2,1)} %select_select_fusion), calls=%async_computation.1 | async-start | bytes 8388608 | tf_op jit(solution)/shard_map/all_to_all | solution.py:72
  100.7 0.1 reshape.159
  100.8 97.7 %all-to-all-done.1 = bf16[16,64,2048]{2,1,0:T(8,128)(2,1)} async-done(((bf16[16,64,2048]{2,1,0:T(8,128)(2,1)}), bf16[16,64,2048]{2,1,0:T(8,128)(2,1)}, u32[]{:S(2)}, u32[]{:S(2)}) %all-to-all-start.1) | async-done | bytes 4194336 | tf_op jit(solution)/shard_map/all_to_all | solution.py:72
  198.5 5.7 %fusion.19 = f32[768,2048]{1,0:T(8,128)S(1)} fusion(bf16[1024,2048]{1,0:T(8,128)(2,1)} %bitcast.8, bf16[1,1,768,1024]{3,2,1,0:T(8,128)(2,1)} %param.10, f32[1024]{0:T(1024)S(1)} %reshape.159), kind=kOutput, calls=%fused_computation.31 | convolution fusion | flops 3223584768 | bytes 12062720 | tf_op jit(solution)/shard_map/dot_general | solution.py:91
  204.2 0.0 copy-start.1
  204.2 0.0 copy-start.2
  204.2 2.6 slice_select_fusion
  206.8 1.5 copy-done.1
  208.4 0.0 copy-start.3
  208.4 2.3 collective-permute-start
  210.7 0.0 copy-done.2
  210.7 0.2 convert_bitcast_fusion.1
  210.9 1.3 collective-permute-start.1
  212.2 100.5 %collective-permute-done.1 = bf16[768,1024]{1,0:T(8,128)(2,1)S(1)} collective-permute-done((bf16[768,1024]{1,0:T(8,128)(2,1)S(1)}, bf16[768,1024]{1,0:T(8,128)(2,1)S(1)}, u32[]{:S(2)}, u32[]{:S(2)}) %collective-permute-start.1) | collective-permute-done | bytes 1572896 | tf_op jit(solution)/shard_map/ppermute | solution.py:15
  312.8 0.0 copy-done.3
  312.8 5.6 %fusion.2 = f32[1024]{0:T(1024)S(1)} fusion(bf16[1,1,768,1024]{3,2,1,0:T(8,128)(2,1)S(1)} %copy-done.3, bf16[1024,2048]{1,0:T(8,128)(2,1)} %bitcast.8, bf16[768,1024]{1,0:T(8,128)(2,1)S(1)} %collective-permute-done.1, bf16[768,1024]{1,0:T(8,128)(2,1)S(1)} %convert_bitcast_fusion.1, pred[]{:T(512)S(6)} %lt.54), kind=kOutput, calls=%fused_computation.11 | convolution fusion | flops 3237739520 | bytes 8916993 | tf_op jit(solution)/shard_map/rd,hd->hr/dot_general | solution.py:42
  318.4 0.7 all_to_all.18
  319.1 3.8 %all-to-all-start.2 = ((f32[16,1,64]{2,1,0:T(1,128)}), f32[16,1,64]{2,1,0:T(1,128)S(1)}, u32[]{:S(2)}, u32[]{:S(2)}) async-start(f32[16,1,64]{2,1,0:T(1,128)} %all_to_all.18), calls=%async_computation.2 | async-start | bytes 16384 | tf_op jit(solution)/shard_map/all_to_all | solution.py:96
  322.9 9.9 %all-to-all-done.2 = f32[16,1,64]{2,1,0:T(1,128)S(1)} async-done(((f32[16,1,64]{2,1,0:T(1,128)}), f32[16,1,64]{2,1,0:T(1,128)S(1)}, u32[]{:S(2)}, u32[]{:S(2)}) %all-to-all-start.2) | async-done | bytes 4128 | tf_op jit(solution)/shard_map/all_to_all | solution.py:96
  332.8 0.5 broadcast.142
  333.3 0.7 reduce.9
  334.0 0.1 reshape.158
  334.1 16.7 %gather_fusion.1 = f32[4096]{0:T(1024)S(1)} fusion(f32[1024]{0:T(1024)S(1)} %reshape.158, s32[4096]{0:T(1024)S(1)} %broadcast_clamp_fusion), kind=kCustom, calls=%fused_computation.1 | custom fusion | bytes 49152 | tf_op jit(solution)/shard_map/gather | solution.py:99
  350.7 0.2 gather.14
  350.9 0.7 copy.34
  351.7 0.0 collective-permute-done
  351.7 8.0 %fusion.16 = f32[1,1,768,1024]{3,2,1,0:T(8,128)} fusion(f32[1,1,768,1024]{3,2,1,0:T(8,128)} %param.11, bf16[1,1,768,1024]{3,2,1,0:T(8,128)(2,1)} %param.13, f32[768,1024]{1,0:T(8,128)} %collective-permute-done, bf16[1,1,768,1024]{3,2,1,0:T(8,128)(2,1)} %param.12, f32[768,2048]{1,0:T(8,128)} %copy-done.1, pred[]{:T(512)S(6)} %lt.54), kind=kLoop, calls=%fused_computation.27 | loop fusion | flops 13369344 | bytes 18874368 | tf_op jit(solution)/shard_map/broadcast_in_dim | solution.py:106
  (11 shorter events, 0.2 us)
Async XLA Ops:
  0.6 80.5 %copy-start = (bf16[1,512,2048]{2,1,0:T(8,128)(2,1)S(1)}, bf16[1,512,2048]{2,1,0:T(8,128)(2,1)}, u32[]{:S(2)}) copy-start(bf16[1,512,2048]{2,1,0:T(8,128)(2,1)} %param.7) | copy-start | bytes 6291460
  36.6 54.4 %all-to-all-start = ((bf16[16,1,64]{2,1,0:T(2,128)(2,1)}), bf16[16,1,64]{2,1,0:T(2,128)(2,1)S(1)}, u32[]{:S(2)}, u32[]{:S(2)}) async-start(bf16[16,1,64]{2,1,0:T(2,128)(2,1)} %all_to_all.20), calls=%async_computation | async-start | bytes 16384 | tf_op jit(solution)/shard_map/all_to_all | solution.py:73
  91.0 107.5 %all-to-all-start.1 = ((bf16[16,64,2048]{2,1,0:T(8,128)(2,1)}), bf16[16,64,2048]{2,1,0:T(8,128)(2,1)}, u32[]{:S(2)}, u32[]{:S(2)}) async-start(bf16[16,64,2048]{2,1,0:T(8,128)(2,1)} %select_select_fusion), calls=%async_computation.1 | async-start | bytes 8388608 | tf_op jit(solution)/shard_map/all_to_all | solution.py:72
  204.2 4.2 %copy-start.1 = (f32[768,2048]{1,0:T(8,128)}, f32[768,2048]{1,0:T(8,128)S(1)}, u32[]{:S(2)}) copy-start(f32[768,2048]{1,0:T(8,128)S(1)} %fusion.19) | copy-start | bytes 18874372
  204.2 6.5 %copy-start.2 = (f32[1,1,768,1024]{3,2,1,0:T(8,128)S(1)}, f32[1,1,768,1024]{3,2,1,0:T(8,128)}, u32[]{:S(2)}) copy-start(f32[1,1,768,1024]{3,2,1,0:T(8,128)} %param.11) | copy-start | bytes 9437188
  208.4 104.4 %copy-start.3 = (bf16[1,1,768,1024]{3,2,1,0:T(8,128)(2,1)S(1)}, bf16[1,1,768,1024]{3,2,1,0:T(8,128)(2,1)}, u32[]{:S(2)}) copy-start(bf16[1,1,768,1024]{3,2,1,0:T(8,128)(2,1)} %param.10) | copy-start | bytes 4718596
  208.4 143.3 %collective-permute-start = (f32[768,1024]{1,0:T(8,128)}, f32[768,1024]{1,0:T(8,128)}, u32[]{:S(2)}, u32[]{:S(2)}) collective-permute-start(f32[768,1024]{1,0:T(8,128)} %slice_select_fusion), channel_id=1, source_target_pairs={{0,128},{16,144},{32,160},{48,176},{64,192},{80,208},{96,224},{112... | collective-permute-start | bytes 9437192 | tf_op jit(solution)/shard_map/ppermute | solution.py:15
  210.9 101.9 %collective-permute-start.1 = (bf16[768,1024]{1,0:T(8,128)(2,1)S(1)}, bf16[768,1024]{1,0:T(8,128)(2,1)S(1)}, u32[]{:S(2)}, u32[]{:S(2)}) collective-permute-start(bf16[768,1024]{1,0:T(8,128)(2,1)S(1)} %convert_bitcast_fusion.1), channel_id=1, source_target_pairs={{0,128},{16,144},{32,160},{48,176},{64,192},{80,208},{96,224},{112... | collective-permute-start | bytes 4718600 | tf_op jit(solution)/shard_map/ppermute | solution.py:15
  319.1 13.7 %all-to-all-start.2 = ((f32[16,1,64]{2,1,0:T(1,128)}), f32[16,1,64]{2,1,0:T(1,128)S(1)}, u32[]{:S(2)}, u32[]{:S(2)}) async-start(f32[16,1,64]{2,1,0:T(1,128)} %all_to_all.18), calls=%async_computation.2 | async-start | bytes 16384 | tf_op jit(solution)/shard_map/all_to_all | solution.py:96
where the time goes:
time: 360 us
  waiting for transfers between devices  208 us (58%)
  local copies, waits for them, and re-layouts  92 us (26%)
  starting transfers between devices  28.1 us (8%)
  other arithmetic  19.2 us (5%)
  matrix products  11.3 us (3%)
    ppermute x2, waiting for transfers between devices, swapped(): lax.ppermute(array, axis, [(i, i ^ 1 << distance) for i in range(lax.axis...  101 us
    all_to_all x1, waiting for transfers between devices, local(): lax.all_to_all(picked, 'ep', split_axis=0, concat_axis=0, tiled=True)  97.7 us
    scatter x1, local copies, waits for them, and re-layouts, local(): jnp.zeros((slot_count,), jnp.bfloat16).at[flat]  28.5 us
    scatter x1, local copies, waits for them, and re-layouts, local(): live = jnp.zeros((slot_count,), jnp.bool_).at[flat].set(True, mode='drop')  17.6 us
    gather x2, local copies, waits for them, and re-layouts, local(): chosen = back.reshape(-1)[jnp.minimum(flat, slot_count - 1)]  16.8 us
    scatter x1, local copies, waits for them, and re-layouts, local(): jnp.zeros((slot_count,), jnp.int32).at[flat].set(token_index, mode='drop')  15.5 us
    all_to_all x1, starting transfers between devices, local(): lax.all_to_all(slot_weight.reshape(group, capacity), 'ep', split_axis=0,...  11 us
    all_to_all x1, waiting for transfers between devices, local(): lax.all_to_all(score.reshape(group, capacity), 'ep', split_axis=0, concat...  9.92 us
  transfers between devices with their start and end apart: 5, of which 3 were waited for; matrix products, arithmetic and copies ran while one was open for 19% of the time, Pallas kernels for 0%

commit v1 on v0

v1 whole, which is shorter than its diff:
```python
import functools

import jax
import jax.numpy as jnp
from jax import lax
from jax.experimental import pallas as pl
from jax.experimental.pallas import tpu as pltpu
from jax.sharding import PartitionSpec as P

beta_first = 0.9
beta_second = 0.95
adam_eps = 1e-08
decay_rate = 0.1
first_fix = 1.0 - 0.9**10
second_fix = 1.0 - 0.95**10

MESH = pl.DeviceIdType.MESH
F32 = jnp.float32
BF16 = jnp.bfloat16

PIECES = (("far", 0, 512), ("far", 512, 512), ("own", 0, 512), ("own", 512, 512))
ROUTES = tuple(
    (dz, dx) for dz in (4, 3, -3, 2, -2, 1, -1, 0) for dx in (1, 0) if (dz, dx) != (0, 0)
)


def split_three(x):
    high = x.astype(BF16)
    rest = x - high.astype(F32)
    middle = rest.astype(BF16)
    low = (rest - middle.astype(F32)).astype(BF16)
    return high, middle, low


def contract_last(a, b):
    return lax.dot_general(a, b, (((1,), (1,)), ((), ())), preferred_element_type=F32)


def kernel(
    ids_ref, rw_ref, tok_hbm, hid_hbm, mas_hbm, mom_hbm, sec_hbm, upd_hbm, rg_ref,
    toks, sends, recvs, onehot, hid, hid_t, scaled, mas, mom, sec, own_w, far_w, v_buf, acc,
    g_send, g_recv, out, w_send, w_recv, s_send, s_recv,
    tok_sem, in_sem, row_ssem, row_rsem, w_ssem, w_rsem, s_ssem, s_rsem, y_ssem, y_rsem, out_sem,
):
    group, cap = 16, 64
    toks_n = ids_ref.shape[1]
    hid_n, slots = hid.shape
    half = mas.shape[1]
    section = lax.axis_index("section")
    me = lax.axis_index("ep")
    count = lax.axis_size("section")
    mirror = lax.rem(section + count // 2, count)
    lower = (section < count // 2).astype(jnp.int32)
    offsets = {"far": lower * half, "own": (1 - lower) * half}
    z, xh = me // 2, me % 2

    tok_copies = []
    for p, (kind, start, width) in enumerate(PIECES):
        column = pl.multiple_of(offsets[kind] + start, 128)
        tok_copies.append(
            pltpu.make_async_copy(tok_hbm.at[:, pl.ds(column, width)], toks[p], tok_sem.at[p])
        )
    mas_copy = pltpu.make_async_copy(mas_hbm, mas, in_sem.at[0])
    hid_copy = pltpu.make_async_copy(hid_hbm, hid, in_sem.at[1])
    mom_copy = pltpu.make_async_copy(mom_hbm, mom, in_sem.at[2])
    sec_copy = pltpu.make_async_copy(sec_hbm, sec, in_sem.at[3])
    tok_copies[0].start()
    mas_copy.start()
    for copy in tok_copies[1:]:
        copy.start()
    hid_copy.start()
    mom_copy.start()
    sec_copy.start()

    peers = [
        (section, lax.rem(z + dz + 8, 8) * 2 + (lax.rem(xh + dx, 2))) for dz, dx in ROUTES
    ]
    barrier = pltpu.get_barrier_semaphore()
    for peer in peers:
        pl.semaphore_signal(barrier, inc=1, device_id=peer, device_id_type=MESH)
    pl.semaphore_signal(barrier, inc=1, device_id=(mirror, me), device_id_type=MESH)

    ids = ids_ref[...]
    weights = rw_ref[...].astype(F32)
    expert = lax.broadcasted_iota(jnp.int32, (group, toks_n), 0)
    member = jnp.zeros((group, toks_n), F32)
    weight = jnp.zeros((group, toks_n), F32)
    for k in range(ids.shape[0]):
        named = ids[k : k + 1, :] == expert
        member = jnp.where(named, 1.0, member)
        weight = jnp.where(named, weights[k : k + 1, :], weight)
    before = (
        lax.broadcasted_iota(jnp.int32, (toks_n, toks_n), 0)
        < lax.broadcasted_iota(jnp.int32, (toks_n, toks_n), 1)
    )
    rank = jnp.dot(
        member.astype(BF16), before.astype(F32).astype(BF16), preferred_element_type=F32
    ).astype(jnp.int32)
    rank = jnp.where(member > 0.0, rank, -1)
    slot = lax.broadcasted_iota(jnp.int32, (cap, toks_n), 0)
    for e in range(group):
        onehot[e * cap : (e + 1) * cap, :] = jnp.where(
            rank[e : e + 1, :] == slot, 1.0, 0.0
        ).astype(BF16)

    def build(p):
        @pl.loop(0, slots // 256)
        def _(b):
            rows = pl.ds(pl.multiple_of(b * 256, 256), 256)
            sends[p][rows, :] = jnp.dot(
                onehot[rows, :], toks[p][...], preferred_element_type=F32
            ).astype(BF16)

        mine = pl.ds(pl.multiple_of(me * cap, cap), cap)
        recvs[p][mine, :] = sends[p][mine, :]

    def row_copy(p, peer):
        there = pl.ds(pl.multiple_of(peer[1] * cap, cap), cap)
        mine = pl.ds(pl.multiple_of(me * cap, cap), cap)
        return pltpu.make_async_remote_copy(
            src_ref=sends[p].at[there, :],
            dst_ref=recvs[p].at[mine, :],
            send_sem=row_ssem.at[p, peer[1]],
            recv_sem=row_rsem.at[p, me],
            device_id=peer,
            device_id_type=MESH,
        )

    def row_arrival(p, peer):
        there = pl.ds(pl.multiple_of(peer[1] * cap, cap), cap)
        return pltpu.make_async_remote_copy(
            src_ref=sends[p].at[there, :],
            dst_ref=recvs[p].at[there, :],
            send_sem=row_ssem.at[p, peer[1]],
            recv_sem=row_rsem.at[p, peer[1]],
            device_id=peer,
            device_id_type=MESH,
        )

    tok_copies[0].wait()
    build(0)
    pl.semaphore_wait(barrier, len(peers) + 1)
    for peer in peers:
        row_copy(0, peer).start()

    spread = contract_last(weight.astype(BF16), onehot[...])
    row = lax.broadcasted_iota(jnp.int32, (group, 128), 0)
    lane = lax.broadcasted_iota(jnp.int32, (group, 128), 1)
    packed = jnp.zeros((group, 128), F32)
    for q in range(slots // 128):
        packed = jnp.where(row // 2 == q, spread[:, q * 128 : (q + 1) * 128], packed)
    packed = jnp.where(lane // cap == row % 2, packed, 0.0)
    packed = packed + pltpu.roll(packed, cap, 1)
    for e in range(group):
        w_send[e] = jnp.broadcast_to(packed[e : e + 1, :], (8, 128))
    w_recv[me] = w_send[me]

    def small_copy(source, target, ssem, rsem, at, peer):
        return pltpu.make_async_remote_copy(
            src_ref=source.at[at],
            dst_ref=target.at[me],
            send_sem=ssem.at[peer[1]],
            recv_sem=rsem.at[me],
            device_id=peer,
            device_id_type=MESH,
        )

    def small_arrival(source, target, ssem, rsem, peer):
        return pltpu.make_async_remote_copy(
            src_ref=source.at[0],
            dst_ref=target.at[peer[1]],
            send_sem=ssem.at[peer[1]],
            recv_sem=rsem.at[peer[1]],
            device_id=peer,
            device_id_type=MESH,
        )

    for peer in peers:
        small_copy(w_send, w_recv, w_ssem, w_rsem, peer[1], peer).start()

    mas_copy.wait()
    own_w[...] = mas[...].astype(BF16)
    far_copy = pltpu.make_async_remote_copy(
        src_ref=own_w, dst_ref=far_w, send_sem=y_ssem.at[0], recv_sem=y_rsem.at[0],
        device_id=(mirror, me), device_id_type=MESH,
    )
    far_copy.start()

    for p in range(1, len(PIECES)):
        tok_copies[p].wait()
        build(p)
        for peer in peers:
            row_copy(p, peer).start()

    hid_copy.wait()

    @pl.loop(0, slots // 256)
    def _(b):
        rows = pl.ds(pl.multiple_of(b * 256, 256), 256)
        hid_t[rows, :] = hid[:, rows].T

    for peer in peers:
        small_arrival(w_send, w_recv, w_ssem, w_rsem, peer).wait_recv()
    lane8 = lax.broadcasted_iota(jnp.int32, (8, 128), 1)
    slot_w = jnp.concatenate(
        [jnp.where(lane8 < cap, w_recv[2 * q], w_recv[2 * q + 1]) for q in range(slots // 128)], 1
    )[0:1, :]

    @pl.loop(0, hid_n // 64)
    def _(b):
        rows = pl.ds(pl.multiple_of(b * 64, 64), 64)
        scaled[rows, :] = (hid[rows, :].astype(F32) * slot_w).astype(BF16)

    def project(p):
        kind, start, width = PIECES[p]
        matrix = own_w if kind == "own" else far_w
        base = start + (half if kind == "own" else 0)

        @pl.loop(0, slots // 256)
        def _(b):
            rows = pl.ds(pl.multiple_of(b * 256, 256), 256)
            v_buf[rows, base : base + width] = jnp.dot(
                hid_t[rows, :], matrix[:, start : start + width], preferred_element_type=F32
            )

    def add_score(p, first):
        kind, start, width = PIECES[p]
        base = start + (half if kind == "own" else 0)

        @pl.loop(0, slots // 64)
        def _(b):
            rows = pl.ds(pl.multiple_of(b * 64, 64), 64)
            product = recvs[p][rows, :].astype(F32) * v_buf[rows, base : base + width]
            partial = product[:, 0:128]
            for q in range(1, width // 128):
                partial = partial + product[:, q * 128 : (q + 1) * 128]
            if first:
                acc[rows, :] = partial
            else:
                acc[rows, :] = acc[rows, :] + partial

    def await_rows(p):
        for peer in peers:
            row_arrival(p, peer).wait_recv()

    def grad_copy(p):
        kind, start, width = PIECES[p]
        return pltpu.make_async_remote_copy(
            src_ref=g_send.at[:, pl.ds(start, width)],
            dst_ref=g_recv.at[:, pl.ds(start, width)],
            send_sem=y_ssem.at[1 + p],
            recv_sem=y_rsem.at[1 + p],
            device_id=(mirror, me),
            device_id_type=MESH,
        )

    far = [p for p, piece in enumerate(PIECES) if piece[0] == "far"]
    own = [p for p, piece in enumerate(PIECES) if piece[0] == "own"]
    for p in own:
        project(p)
    for n, p in enumerate(far):
        kind, start, width = PIECES[p]
        await_rows(p)

        @pl.loop(0, hid_n // 256)
        def _(b):
            rows = pl.ds(pl.multiple_of(b * 256, 256), 256)
            g_send[rows, start : start + width] = jnp.dot(
                scaled[rows, :], recvs[p][...], preferred_element_type=F32
            ).astype(BF16)

        grad_copy(p).start()
        if n == 0:
            far_copy.wait_recv()
        project(p)
        add_score(p, n == 0)

    mom_copy.wait()
    sec_copy.wait()

    def finish(p):
        kind, start, width = PIECES[p]

        @pl.loop(0, hid_n // 128)
        def _(b):
            rows = pl.ds(pl.multiple_of(b * 128, 128), 128)
            cols = slice(start, start + width)
            total = (
                jnp.dot(scaled[rows, :], recvs[p][...], preferred_element_type=F32)
                + g_recv[rows, cols].astype(F32)
            )
            first_new = beta_first * mom[rows, cols].astype(F32) + (1.0 - beta_first) * total
            second_new = (
                beta_second * sec[rows, cols].astype(F32) + (1.0 - beta_second) * total * total
            )
            out[rows, cols] = (
                first_new / first_fix / (jnp.sqrt(second_new / second_fix) + adam_eps)
                + decay_rate * mas[rows, cols]
            )

        copy = pltpu.make_async_copy(
            out.at[:, pl.ds(start, width)], upd_hbm.at[:, pl.ds(start, width)], out_sem.at[p]
        )
        copy.start()
        return copy

    out_copies = []
    for p in own[:-1]:
        await_rows(p)
        add_score(p, False)
        for q in far:
            if PIECES[q][1] == PIECES[p][1]:
                grad_copy(q).wait_recv()
        out_copies.append(finish(p))

    last = own[-1]
    await_rows(last)
    add_score(last, False)
    ones = jnp.ones((8, 128), BF16)
    score = jnp.zeros((8, slots), F32)
    for part in split_three(acc[...]):
        score = score + contract_last(ones, part)
    for q in range(slots // 128):
        s_send[q] = score[:, q * 128 : (q + 1) * 128]
    s_recv[me] = s_send[me // 2]
    for peer in peers:
        small_copy(s_send, s_recv, s_ssem, s_rsem, peer[1] // 2, peer).start()
    for q in far:
        if PIECES[q][1] == PIECES[last][1]:
            grad_copy(q).wait_recv()
    out_copies.append(finish(last))

    for peer in peers:
        small_arrival(s_send, s_recv, s_ssem, s_rsem, peer).wait_recv()
    got = jnp.concatenate([s_recv[e][0:1, :] for e in range(group)], 0)
    mine = lane // cap == xh
    got = jnp.where(mine, got, pltpu.roll(got, cap, 1))
    wide_row = lax.broadcasted_iota(jnp.int32, (group, slots), 0)
    wide_lane = lax.broadcasted_iota(jnp.int32, (group, slots), 1)
    wide = jnp.where(wide_lane // cap == wide_row, jnp.concatenate([got] * (slots // 128), 1), 0.0)
    found = jnp.zeros((group, toks_n), F32)
    for part in split_three(wide):
        found = found + jnp.dot(part, onehot[...], preferred_element_type=F32)
    for k in range(ids.shape[0]):
        rg_ref[k : k + 1, :] = jnp.sum(
            jnp.where(ids[k : k + 1, :] == expert, found, 0.0), axis=0, keepdims=True
        )

    for copy in out_copies:
        copy.wait()
    far_copy.wait_send()
    for p in far:
        grad_copy(p).wait_send()
    for peer in peers:
        for p in range(len(PIECES)):
            row_copy(p, peer).wait_send()
        small_copy(w_send, w_recv, w_ssem, w_rsem, peer[1], peer).wait_send()
        small_copy(s_send, s_recv, s_ssem, s_rsem, peer[1] // 2, peer).wait_send()


def local(grad_out, router_weights, expert_ids, hidden, master, moment, second):
    toks_n, width = grad_out.shape[1:]
    hid_n, slots = hidden.shape[2:]
    half = master.shape[3]
    top = expert_ids.shape[2]
    pieces = len(PIECES)
    dma = pltpu.SemaphoreType.DMA
    hbm = pl.BlockSpec(memory_space=pl.ANY)
    vmem = pl.BlockSpec(memory_space=pltpu.VMEM)
    update, router = pl.pallas_call(
        kernel,
        out_shape=(
            jax.ShapeDtypeStruct((hid_n, half), F32),
            jax.ShapeDtypeStruct((top, toks_n), F32),
        ),
        in_specs=[vmem, vmem, hbm, hbm, hbm, hbm, hbm],
        out_specs=(hbm, vmem),
        scratch_shapes=[
            [pltpu.VMEM((toks_n, w), BF16) for _, _, w in PIECES],
            [pltpu.VMEM((slots, w), BF16) for _, _, w in PIECES],
            [pltpu.VMEM((slots, w), BF16) for _, _, w in PIECES],
            pltpu.VMEM((slots, toks_n), BF16),
            pltpu.VMEM((hid_n, slots), BF16),
            pltpu.VMEM((slots, hid_n), BF16),
            pltpu.VMEM((hid_n, slots), BF16),
            pltpu.VMEM((hid_n, half), F32),
            pltpu.VMEM((hid_n, half), BF16),
            pltpu.VMEM((hid_n, half), BF16),
            pltpu.VMEM((hid_n, half), BF16),
            pltpu.VMEM((hid_n, half), BF16),
            pltpu.VMEM((slots, width), F32),
            pltpu.VMEM((slots, 128), F32),
            pltpu.VMEM((hid_n, half), BF16),
            pltpu.VMEM((hid_n, half), BF16),
            pltpu.VMEM((hid_n, half), F32),
            pltpu.VMEM((16, 8, 128), F32),
            pltpu.VMEM((16, 8, 128), F32),
            pltpu.VMEM((8, 8, 128), F32),
            pltpu.VMEM((16, 8, 128), F32),
            dma((pieces,)),
            dma((4,)),
            dma((pieces, 16)),
            dma((pieces, 16)),
            dma((16,)),
            dma((16,)),
            dma((16,)),
            dma((16,)),
            dma((1 + pieces,)),
            dma((1 + pieces,)),
            dma((pieces,)),
        ],
        compiler_params=pltpu.CompilerParams(
            collective_id=0, has_side_effects=True, vmem_limit_bytes=56 << 20
        ),
    )(
        expert_ids[0].T, router_weights[0].T, grad_out[0], hidden[0, 0], master[0, 0],
        moment[0, 0], second[0, 0],
    )
    return (update[None, None], router.T[None])


def solution(mesh):
    placed = (
        P("section", "ep", None),
        P("section", "ep", None),
        P("section", "ep", None),
        P("section", "ep", None, None),
        P("section", "ep", None, None),
        P("section", "ep", None, None),
        P("section", "ep", None, None),
    )
    return jax.shard_map(
        local,
        mesh=mesh,
        in_specs=placed,
        out_specs=(P("section", "ep", None, None), P("section", "ep", None)),
        check_vma=False,
    )
```

time: 360 us -> 119 us (0.33)
  waiting for transfers between devices: 208 us -> 0 us
  Pallas kernels: 0 us -> 114 us
  local copies, waits for them, and re-layouts: 92 us -> 4.58 us
  starting transfers between devices: 28.1 us -> 0 us
  other arithmetic: 19.2 us -> 0 us
  matrix products: 11.3 us -> 0 us
    pallas_call x0 -> x1, Pallas kernels: none -> 114 us  [local(): pl.pallas_call(kernel, out_shape=(jax.ShapeDtypeStruct((hid_n, half), F32...]
    all_to_all x3 -> x0, waiting for transfers between devices: 108 us -> none  [the longest x1 97.7 us: local(): lax.all_to_all(picked, 'ep', split_axis=0, concat_axis=0, tiled=True)]
    ppermute x2 -> x0, waiting for transfers between devices: 101 us -> none  [swapped(): lax.ppermute(array, axis, [(i, i ^ 1 << distance) for i in range(lax.axis...]
    scatter x3 -> x0, local copies, waits for them, and re-layouts: 61.7 us -> none  [the longest x1 28.5 us: local(): jnp.zeros((slot_count,), jnp.bfloat16).at[flat]]
    all_to_all x3 -> x0, starting transfers between devices: 24.5 us -> none  [the longest x1 11 us: local(): lax.all_to_all(slot_weight.reshape(group, capacity), 'ep', split_axis=0,...]
    gather x3 -> x0, local copies, waits for them, and re-layouts: 22.8 us -> none  [the longest x2 16.8 us: local(): chosen = back.reshape(-1)[jnp.minimum(flat, slot_count - 1)]]
    dot_general x2 -> x0, matrix products: 11.3 us -> none  [the longest x1 5.65 us: local(): grad = jnp.dot(scaled, rows, preferred_element_type=jnp.float32)]
    broadcast_in_dim x1 -> x0, other arithmetic: 7.97 us -> none  [local(): return (update[None, None], router[None])]
  transfers between devices with their start and end apart: 5 -> 0, of which waited for: 3 -> 0; matrix products, arithmetic and copies ran while one was open for 19% -> 0% of each run, Pallas kernels for 0% -> 0%
where the time goes in v1:
time: 119 us
  Pallas kernels  114 us (96%)
  local copies, waits for them, and re-layouts  4.58 us (4%)
    pallas_call x1, Pallas kernels, local(): pl.pallas_call(kernel, out_shape=(jax.ShapeDtypeStruct((hid_n, half), F32...  114 us
    unnamed x4, local copies, waits for them, and re-layouts  4.58 us

profile of v1, /device:TPU:8, one launch (start us, length us, event | category | flops | bytes accessed | tf_op | source)
XLA Modules:
  0.0 119.1 jit_solution(5905419953764718137)
XLA Ops:
  0.6 113.9 %shard_map.86 = (f32[768,1024]{1,0:T(8,128)}, f32[8,512]{1,0:T(8,128)}) custom-call(s32[8,512]{1,0:T(8,128)} %bitcast.21, bf16[8,512]{1,0:T(8,128)(2,1)} %bitcast.23, bf16[512,2048]{1,0:T(8,128)(2,1)} %bitcast.17, bf16[768,1024]{1,0:T(8,128)(2,1)} %bitcast.18, f32[768,1024]{1,0:T(8,128)} %bitcast.16, bf16[768,1024]{1,0:T(8,128)(2,1)} %bitcast.19, ...), custom_call_target="tpu_custom_call" | custom-call | tf_op jit(solution)/shard_map/pallas_call | solution.py:370
  114.5 0.0 copy-start
  114.6 4.0 %copy.11 = f32[1,1,768,1024]{3,2,1,0:T(8,128)} copy(f32[1,1,768,1024]{3,2,1,0:T(8,128)} %bitcast.15) | data formatting | bytes 6291456
  118.5 0.0 copy-done
  118.5 0.6 copy.12
Async XLA Ops:
  114.5 4.0 %copy-start = (f32[8,512]{1,0:T(8,128)S(1)}, f32[8,512]{1,0:T(8,128)}, u32[]{:S(2)}) copy-start(f32[8,512]{1,0:T(8,128)} %get-tuple-element.5) | copy-start | bytes 49156

commit v2 on v1

--- a/solution.py
+++ b/solution.py
@@ -18,18 +18,19 @@
 F32 = jnp.float32
 BF16 = jnp.bfloat16
 
-PIECES = (("far", 0, 512), ("far", 512, 512), ("own", 0, 512), ("own", 512, 512))
+PIECES = (("far", 0, 256), ("far", 256, 768), ("own", 0, 512), ("own", 512, 384), ("own", 896, 128))
 ROUTES = tuple(
-    (dz, dx) for dz in (4, 3, -3, 2, -2, 1, -1, 0) for dx in (1, 0) if (dz, dx) != (0, 0)
+    (dz, dx) for dz in (0, -1, 1, -2, 2, -3, 3, 4) for dx in (0, 1) if (dz, dx) != (0, 0)
 )
 
 
-def split_three(x):
+def split_two(x):
     high = x.astype(BF16)
-    rest = x - high.astype(F32)
-    middle = rest.astype(BF16)
-    low = (rest - middle.astype(F32)).astype(BF16)
-    return high, middle, low
+    return high, (x - high.astype(F32)).astype(BF16)
+
+
+def blocks(start, width):
+    return [(c, min(256, start + width - c)) for c in range(start, start + width, 256)]
 
 
 def contract_last(a, b):
@@ -37,10 +38,10 @@
 
 
 def kernel(
-    ids_ref, rw_ref, tok_hbm, hid_hbm, mas_hbm, mom_hbm, sec_hbm, upd_hbm, rg_ref,
+    ids_ref, rw_ref, tok_hbm, hid_hbm, mas_hbm, mom_hbm, sec_hbm, out, rg_ref,
     toks, sends, recvs, onehot, hid, hid_t, scaled, mas, mom, sec, own_w, far_w, v_buf, acc,
-    g_send, g_recv, out, w_send, w_recv, s_send, s_recv,
-    tok_sem, in_sem, row_ssem, row_rsem, w_ssem, w_rsem, s_ssem, s_rsem, y_ssem, y_rsem, out_sem,
+    g_send, g_recv, fresh, w_send, w_recv, s_send, s_recv,
+    tok_sem, in_sem, row_ssem, row_rsem, w_sem, s_sem, y_ssem, y_rsem,
 ):
     group, cap = 16, 64
     toks_n = ids_ref.shape[1]
@@ -89,13 +90,21 @@
         named = ids[k : k + 1, :] == expert
         member = jnp.where(named, 1.0, member)
         weight = jnp.where(named, weights[k : k + 1, :], weight)
-    before = (
-        lax.broadcasted_iota(jnp.int32, (toks_n, toks_n), 0)
-        < lax.broadcasted_iota(jnp.int32, (toks_n, toks_n), 1)
-    )
-    rank = jnp.dot(
-        member.astype(BF16), before.astype(F32).astype(BF16), preferred_element_type=F32
-    ).astype(jnp.int32)
+    parts = [member[:, b * 128 : (b + 1) * 128] for b in range(toks_n // 128)]
+    column = lax.broadcasted_iota(jnp.int32, (128, 256), 1)
+    before = (lax.broadcasted_iota(jnp.int32, (128, 256), 0) < column) | (column >= 128)
+    counted = jnp.dot(
+        jnp.concatenate(parts, 0).astype(BF16),
+        jnp.where(before, 1.0, 0.0).astype(BF16),
+        preferred_element_type=F32,
+    )
+    passed = jnp.zeros((group, 128), F32)
+    ranks = []
+    for b in range(toks_n // 128):
+        rows = slice(b * group, (b + 1) * group)
+        ranks.append(counted[rows, :128] + passed)
+        passed = passed + counted[rows, 128:]
+    rank = jnp.concatenate(ranks, 1).astype(jnp.int32)
     rank = jnp.where(member > 0.0, rank, -1)
     slot = lax.broadcasted_iota(jnp.int32, (cap, toks_n), 0)
     for e in range(group):
@@ -120,20 +129,20 @@
         return pltpu.make_async_remote_copy(
             src_ref=sends[p].at[there, :],
             dst_ref=recvs[p].at[mine, :],
-            send_sem=row_ssem.at[p, peer[1]],
-            recv_sem=row_rsem.at[p, me],
+            send_sem=row_ssem.at[p],
+            recv_sem=row_rsem.at[p],
             device_id=peer,
             device_id_type=MESH,
         )
 
-    def row_arrival(p, peer):
-        there = pl.ds(pl.multiple_of(peer[1] * cap, cap), cap)
+    def all_rows(p):
+        rows = pl.ds(0, len(peers) * cap)
         return pltpu.make_async_remote_copy(
-            src_ref=sends[p].at[there, :],
-            dst_ref=recvs[p].at[there, :],
-            send_sem=row_ssem.at[p, peer[1]],
-            recv_sem=row_rsem.at[p, peer[1]],
-            device_id=peer,
+            src_ref=sends[p].at[rows, :],
+            dst_ref=recvs[p].at[rows, :],
+            send_sem=row_ssem.at[p],
+            recv_sem=row_rsem.at[p],
+            device_id=peers[0],
             device_id_type=MESH,
         )
 
@@ -155,28 +164,28 @@
         w_send[e] = jnp.broadcast_to(packed[e : e + 1, :], (8, 128))
     w_recv[me] = w_send[me]
 
-    def small_copy(source, target, ssem, rsem, at, peer):
+    def small_copy(source, target, sems, at, peer):
         return pltpu.make_async_remote_copy(
             src_ref=source.at[at],
             dst_ref=target.at[me],
-            send_sem=ssem.at[peer[1]],
-            recv_sem=rsem.at[me],
+            send_sem=sems.at[0],
+            recv_sem=sems.at[1],
             device_id=peer,
             device_id_type=MESH,
         )
 
-    def small_arrival(source, target, ssem, rsem, peer):
+    def all_small(target, sems):
         return pltpu.make_async_remote_copy(
-            src_ref=source.at[0],
-            dst_ref=target.at[peer[1]],
-            send_sem=ssem.at[peer[1]],
-            recv_sem=rsem.at[peer[1]],
-            device_id=peer,
+            src_ref=target.at[pl.ds(0, len(peers))],
+            dst_ref=target.at[pl.ds(0, len(peers))],
+            send_sem=sems.at[0],
+            recv_sem=sems.at[1],
+            device_id=peers[0],
             device_id_type=MESH,
         )
 
     for peer in peers:
-        small_copy(w_send, w_recv, w_ssem, w_rsem, peer[1], peer).start()
+        small_copy(w_send, w_recv, w_sem, peer[1], peer).start()
 
     mas_copy.wait()
     own_w[...] = mas[...].astype(BF16)
@@ -199,8 +208,7 @@
         rows = pl.ds(pl.multiple_of(b * 256, 256), 256)
         hid_t[rows, :] = hid[:, rows].T
 
-    for peer in peers:
-        small_arrival(w_send, w_recv, w_ssem, w_rsem, peer).wait_recv()
+    all_small(w_recv, w_sem).wait_recv()
     lane8 = lax.broadcasted_iota(jnp.int32, (8, 128), 1)
     slot_w = jnp.concatenate(
         [jnp.where(lane8 < cap, w_recv[2 * q], w_recv[2 * q + 1]) for q in range(slots // 128)], 1
@@ -240,8 +248,7 @@
                 acc[rows, :] = acc[rows, :] + partial
 
     def await_rows(p):
-        for peer in peers:
-            row_arrival(p, peer).wait_recv()
+        all_rows(p).wait_recv()
 
     def grad_copy(p):
         kind, start, width = PIECES[p]
@@ -278,84 +285,73 @@
     mom_copy.wait()
     sec_copy.wait()
 
+    arrived = []
+
     def finish(p):
         kind, start, width = PIECES[p]
-
-        @pl.loop(0, hid_n // 128)
-        def _(b):
-            rows = pl.ds(pl.multiple_of(b * 128, 128), 128)
-            cols = slice(start, start + width)
-            total = (
-                jnp.dot(scaled[rows, :], recvs[p][...], preferred_element_type=F32)
-                + g_recv[rows, cols].astype(F32)
+        for q in far:
+            if q not in arrived and PIECES[q][1] < start + width:
+                grad_copy(q).wait_recv()
+                arrived.append(q)
+        for c, n in blocks(0, width):
+            fresh[:, :n] = jnp.dot(
+                scaled[...], recvs[p][:, c : c + n], preferred_element_type=F32
             )
-            first_new = beta_first * mom[rows, cols].astype(F32) + (1.0 - beta_first) * total
-            second_new = (
-                beta_second * sec[rows, cols].astype(F32) + (1.0 - beta_second) * total * total
-            )
-            out[rows, cols] = (
-                first_new / first_fix / (jnp.sqrt(second_new / second_fix) + adam_eps)
-                + decay_rate * mas[rows, cols]
-            )
-
-        copy = pltpu.make_async_copy(
-            out.at[:, pl.ds(start, width)], upd_hbm.at[:, pl.ds(start, width)], out_sem.at[p]
-        )
-        copy.start()
-        return copy
-
-    out_copies = []
+
+            @pl.loop(0, hid_n // 64)
+            def _(b):
+                rows = pl.ds(pl.multiple_of(b * 64, 64), 64)
+                cols = slice(start + c, start + c + n)
+                total = fresh[rows, :n] + g_recv[rows, cols].astype(F32)
+                first_new = (beta_first / first_fix) * mom[rows, cols].astype(F32) + (
+                    (1.0 - beta_first) / first_fix
+                ) * total
+                second_new = (beta_second / second_fix) * sec[rows, cols].astype(F32) + (
+                    (1.0 - beta_second) / second_fix
+                ) * (total * total)
+                out[rows, cols] = (
+                    first_new / (jnp.sqrt(second_new) + adam_eps) + decay_rate * mas[rows, cols]
+                )
+
     for p in own[:-1]:
         await_rows(p)
         add_score(p, False)
-        for q in far:
-            if PIECES[q][1] == PIECES[p][1]:
-                grad_copy(q).wait_recv()
-        out_copies.append(finish(p))
+        finish(p)
 
     last = own[-1]
     await_rows(last)
     add_score(last, False)
-    ones = jnp.ones((8, 128), BF16)
-    score = jnp.zeros((8, slots), F32)
-    for part in split_three(acc[...]):
-        score = score + contract_last(ones, part)
+    score = contract_last(jnp.ones((8, 256), BF16), jnp.concatenate(split_two(acc[...]), 1))
     for q in range(slots // 128):
         s_send[q] = score[:, q * 128 : (q + 1) * 128]
     s_recv[me] = s_send[me // 2]
     for peer in peers:
-        small_copy(s_send, s_recv, s_ssem, s_rsem, peer[1] // 2, peer).start()
-    for q in far:
-        if PIECES[q][1] == PIECES[last][1]:
-            grad_copy(q).wait_recv()
-    out_copies.append(finish(last))
-
-    for peer in peers:
-        small_arrival(s_send, s_recv, s_ssem, s_rsem, peer).wait_recv()
+        small_copy(s_send, s_recv, s_sem, peer[1] // 2, peer).start()
+    finish(last)
+
+    all_small(s_recv, s_sem).wait_recv()
     got = jnp.concatenate([s_recv[e][0:1, :] for e in range(group)], 0)
     mine = lane // cap == xh
     got = jnp.where(mine, got, pltpu.roll(got, cap, 1))
-    wide_row = lax.broadcasted_iota(jnp.int32, (group, slots), 0)
-    wide_lane = lax.broadcasted_iota(jnp.int32, (group, slots), 1)
-    wide = jnp.where(wide_lane // cap == wide_row, jnp.concatenate([got] * (slots // 128), 1), 0.0)
-    found = jnp.zeros((group, toks_n), F32)
-    for part in split_three(wide):
-        found = found + jnp.dot(part, onehot[...], preferred_element_type=F32)
+    found = jnp.concatenate(
+        [
+            jnp.take_along_axis(got, jnp.maximum(rank[:, b * 128 : (b + 1) * 128], 0), axis=1)
+            for b in range(toks_n // 128)
+        ],
+        1,
+    )
     for k in range(ids.shape[0]):
         rg_ref[k : k + 1, :] = jnp.sum(
             jnp.where(ids[k : k + 1, :] == expert, found, 0.0), axis=0, keepdims=True
         )
 
-    for copy in out_copies:
-        copy.wait()
     far_copy.wait_send()
     for p in far:
         grad_copy(p).wait_send()
-    for peer in peers:
-        for p in range(len(PIECES)):
-            row_copy(p, peer).wait_send()
-        small_copy(w_send, w_recv, w_ssem, w_rsem, peer[1], peer).wait_send()
-        small_copy(s_send, s_recv, s_ssem, s_rsem, peer[1] // 2, peer).wait_send()
+    for p in range(len(PIECES)):
+        all_rows(p).wait_send()
+    all_small(w_recv, w_sem).wait_send()
+    all_small(s_recv, s_sem).wait_send()
 
 
 def local(grad_out, router_weights, expert_ids, hidden, master, moment, second):
@@ -370,11 +366,11 @@
     update, router = pl.pallas_call(
         kernel,
         out_shape=(
-            jax.ShapeDtypeStruct((hid_n, half), F32),
-            jax.ShapeDtypeStruct((top, toks_n), F32),
+            pltpu.VMEM((hid_n, half), F32),
+            pltpu.VMEM((top, toks_n), F32),
         ),
         in_specs=[vmem, vmem, hbm, hbm, hbm, hbm, hbm],
-        out_specs=(hbm, vmem),
+        out_specs=(vmem, vmem),
         scratch_shapes=[
             [pltpu.VMEM((toks_n, w), BF16) for _, _, w in PIECES],
             [pltpu.VMEM((slots, w), BF16) for _, _, w in PIECES],
@@ -392,25 +388,22 @@
             pltpu.VMEM((slots, 128), F32),
             pltpu.VMEM((hid_n, half), BF16),
             pltpu.VMEM((hid_n, half), BF16),
-            pltpu.VMEM((hid_n, half), F32),
+            pltpu.VMEM((hid_n, 256), F32),
             pltpu.VMEM((16, 8, 128), F32),
             pltpu.VMEM((16, 8, 128), F32),
             pltpu.VMEM((8, 8, 128), F32),
             pltpu.VMEM((16, 8, 128), F32),
             dma((pieces,)),
             dma((4,)),
-            dma((pieces, 16)),
-            dma((pieces, 16)),
-            dma((16,)),
-            dma((16,)),
-            dma((16,)),
-            dma((16,)),
+            dma((pieces,)),
+            dma((pieces,)),
+            dma((2,)),
+            dma((2,)),
             dma((1 + pieces,)),
             dma((1 + pieces,)),
-            dma((pieces,)),
         ],
         compiler_params=pltpu.CompilerParams(
-            collective_id=0, has_side_effects=True, vmem_limit_bytes=56 << 20
+            collective_id=0, has_side_effects=True, vmem_limit_bytes=58 << 20
         ),
     )(
         expert_ids[0].T, router_weights[0].T, grad_out[0], hidden[0, 0], master[0, 0],

time: 119 us -> 117 us (0.983)
  local copies, waits for them, and re-layouts: 4.58 us -> 2.27 us
    unnamed x4 -> x2, local copies, waits for them, and re-layouts: 4.58 us -> 2.27 us
where the time goes in v2:
time: 117 us; the launch traced here: 116 us
  Pallas kernels  113 us (97%)
  local copies, waits for them, and re-layouts  2.27 us (2%)
    pallas_call x1, Pallas kernels, local(): pl.pallas_call(kernel, out_shape=(pltpu.VMEM((hid_n, half), F32), pltpu.V...  113 us

profile of v2, /device:TPU:8, one launch (start us, length us, event | category | flops | bytes accessed | tf_op | source)
XLA Modules:
  0.0 116.4 jit_solution(10239287506038285811)
XLA Ops:
  0.6 113.5 %shard_map.86 = (f32[768,1024]{1,0:T(8,128)S(1)}, f32[8,512]{1,0:T(8,128)S(1)}) custom-call(s32[8,512]{1,0:T(8,128)} %bitcast.22, bf16[8,512]{1,0:T(8,128)(2,1)} %bitcast.23, bf16[512,2048]{1,0:T(8,128)(2,1)} %bitcast.18, bf16[768,1024]{1,0:T(8,128)(2,1)} %bitcast.19, f32[768,1024]{1,0:T(8,128)} %bitcast.17, bf16[768,1024]{1,0:T(8,128)(2,1)} %bitcast.20, ...), custom_call_target="tpu_custom_call" | custom-call | tf_op jit(solution)/shard_map/pallas_call | solution.py:366
  114.1 1.7 %copy.11 = f32[1,1,768,1024]{3,2,1,0:T(8,128)} copy(f32[1,1,768,1024]{3,2,1,0:T(8,128)S(1)} %bitcast.15) | data formatting | bytes 6291456
  115.8 0.6 copy.12

commit v3 on v2

--- a/solution.py
+++ b/solution.py
@@ -18,9 +18,10 @@
 F32 = jnp.float32
 BF16 = jnp.bfloat16
 
-PIECES = (("far", 0, 256), ("far", 256, 768), ("own", 0, 512), ("own", 512, 384), ("own", 896, 128))
+PIECES = (("far", 0, 512), ("far", 512, 512), ("own", 0, 512), ("own", 512, 256), ("own", 768, 256))
+GROUPS = ((4, 3, -3), (2, -2), (1, -1, 0))
 ROUTES = tuple(
-    (dz, dx) for dz in (0, -1, 1, -2, 2, -3, 3, 4) for dx in (0, 1) if (dz, dx) != (0, 0)
+    (dz, dx) for dz in (4, 3, -3, 2, -2, 1, -1, 0) for dx in (0, 1) if (dz, dx) != (0, 0)
 )
 
 
@@ -76,6 +77,9 @@
     peers = [
         (section, lax.rem(z + dz + 8, 8) * 2 + (lax.rem(xh + dx, 2))) for dz, dx in ROUTES
     ]
+    bands = [
+        [peer for (dz, _), peer in zip(ROUTES, peers) if dz in group_dz] for group_dz in GROUPS
+    ]
     barrier = pltpu.get_barrier_semaphore()
     for peer in peers:
         pl.semaphore_signal(barrier, inc=1, device_id=peer, device_id_type=MESH)
@@ -123,25 +127,27 @@
         mine = pl.ds(pl.multiple_of(me * cap, cap), cap)
         recvs[p][mine, :] = sends[p][mine, :]
 
-    def row_copy(p, peer):
+    def row_copy(p, peer, sem=None):
+        sem = p if sem is None else sem
         there = pl.ds(pl.multiple_of(peer[1] * cap, cap), cap)
         mine = pl.ds(pl.multiple_of(me * cap, cap), cap)
         return pltpu.make_async_remote_copy(
             src_ref=sends[p].at[there, :],
             dst_ref=recvs[p].at[mine, :],
-            send_sem=row_ssem.at[p],
-            recv_sem=row_rsem.at[p],
+            send_sem=row_ssem.at[sem],
+            recv_sem=row_rsem.at[sem],
             device_id=peer,
             device_id_type=MESH,
         )
 
-    def all_rows(p):
-        rows = pl.ds(0, len(peers) * cap)
+    def all_rows(p, sem=None, number=None):
+        sem = p if sem is None else sem
+        rows = pl.ds(0, (len(peers) if number is None else number) * cap)
         return pltpu.make_async_remote_copy(
             src_ref=sends[p].at[rows, :],
             dst_ref=recvs[p].at[rows, :],
-            send_sem=row_ssem.at[p],
-            recv_sem=row_rsem.at[p],
+            send_sem=row_ssem.at[sem],
+            recv_sem=row_rsem.at[sem],
             device_id=peers[0],
             device_id_type=MESH,
         )
@@ -198,8 +204,13 @@
     for p in range(1, len(PIECES)):
         tok_copies[p].wait()
         build(p)
-        for peer in peers:
-            row_copy(p, peer).start()
+        if p < len(PIECES) - 1:
+            for peer in peers:
+                row_copy(p, peer).start()
+        else:
+            for g, band in enumerate(bands):
+                for peer in band:
+                    row_copy(p, peer, p + g).start()
 
     hid_copy.wait()
 
@@ -319,20 +330,27 @@
         finish(p)
 
     last = own[-1]
-    await_rows(last)
-    add_score(last, False)
-    score = contract_last(jnp.ones((8, 256), BF16), jnp.concatenate(split_two(acc[...]), 1))
-    for q in range(slots // 128):
-        s_send[q] = score[:, q * 128 : (q + 1) * 128]
-    s_recv[me] = s_send[me // 2]
-    for peer in peers:
-        small_copy(s_send, s_recv, s_sem, peer[1] // 2, peer).start()
+    base, width = PIECES[last][1] + half, PIECES[last][2]
+
+    def score_of(e):
+        rows = pl.ds(pl.multiple_of(e * cap, cap), cap)
+        product = recvs[last][rows, :].astype(F32) * v_buf[rows, base : base + width]
+        total = acc[rows, :]
+        for q in range(width // 128):
+            total = total + product[:, q * 128 : (q + 1) * 128]
+        line = contract_last(jnp.ones((8, 256), BF16), jnp.concatenate(split_two(total), 1))
+        return jnp.concatenate([line, jnp.zeros((8, 128 - cap), F32)], 1)
+
+    s_recv[me] = score_of(me)
+    for g, band in enumerate(bands):
+        all_rows(last, last + g, len(band)).wait_recv()
+        for peer in band:
+            s_send[peer[1]] = score_of(peer[1])
+            small_copy(s_send, s_recv, s_sem, peer[1], peer).start()
     finish(last)
 
     all_small(s_recv, s_sem).wait_recv()
     got = jnp.concatenate([s_recv[e][0:1, :] for e in range(group)], 0)
-    mine = lane // cap == xh
-    got = jnp.where(mine, got, pltpu.roll(got, cap, 1))
     found = jnp.concatenate(
         [
             jnp.take_along_axis(got, jnp.maximum(rank[:, b * 128 : (b + 1) * 128], 0), axis=1)
@@ -348,8 +366,10 @@
     far_copy.wait_send()
     for p in far:
         grad_copy(p).wait_send()
-    for p in range(len(PIECES)):
+    for p in range(len(PIECES) - 1):
         all_rows(p).wait_send()
+    for g, band in enumerate(bands):
+        all_rows(last, last + g, len(band)).wait_send()
     all_small(w_recv, w_sem).wait_send()
     all_small(s_recv, s_sem).wait_send()
 
@@ -391,12 +411,12 @@
             pltpu.VMEM((hid_n, 256), F32),
             pltpu.VMEM((16, 8, 128), F32),
             pltpu.VMEM((16, 8, 128), F32),
-            pltpu.VMEM((8, 8, 128), F32),
+            pltpu.VMEM((16, 8, 128), F32),
             pltpu.VMEM((16, 8, 128), F32),
             dma((pieces,)),
             dma((4,)),
-            dma((pieces,)),
-            dma((pieces,)),
+            dma((pieces + len(GROUPS) - 1,)),
+            dma((pieces + len(GROUPS) - 1,)),
             dma((2,)),
             dma((2,)),
             dma((1 + pieces,)),

time: 117 us -> 114 us (0.974)
  Pallas kernels: 113 us -> 111 us
    pallas_call x1, Pallas kernels: 113 us -> 111 us  [local(): pl.pallas_call(kernel, out_shape=(pltpu.VMEM((hid_n, half), F32), pltpu.V...]
where the time goes in v3:
time: 114 us; the launch traced here: 113 us
  Pallas kernels  111 us (97%)
  local copies, waits for them, and re-layouts  2.27 us (2%)
    pallas_call x1, Pallas kernels, local(): pl.pallas_call(kernel, out_shape=(pltpu.VMEM((hid_n, half), F32), pltpu.V...  111 us

profile of v3, /device:TPU:8, one launch (start us, length us, event | category | flops | bytes accessed | tf_op | source)
XLA Modules:
  0.0 113.5 jit_solution(12377324089581358848)
XLA Ops:
  0.6 110.5 %shard_map.86 = (f32[768,1024]{1,0:T(8,128)S(1)}, f32[8,512]{1,0:T(8,128)S(1)}) custom-call(s32[8,512]{1,0:T(8,128)} %bitcast.22, bf16[8,512]{1,0:T(8,128)(2,1)} %bitcast.23, bf16[512,2048]{1,0:T(8,128)(2,1)} %bitcast.18, bf16[768,1024]{1,0:T(8,128)(2,1)} %bitcast.19, f32[768,1024]{1,0:T(8,128)} %bitcast.17, bf16[768,1024]{1,0:T(8,128)(2,1)} %bitcast.20, ...), custom_call_target="tpu_custom_call" | custom-call | tf_op jit(solution)/shard_map/pallas_call | solution.py:386
  111.2 1.7 %copy.11 = f32[1,1,768,1024]{3,2,1,0:T(8,128)} copy(f32[1,1,768,1024]{3,2,1,0:T(8,128)S(1)} %bitcast.15) | data formatting | bytes 6291456
  112.9 0.6 copy.12

commit v4 on v3

--- a/solution.py
+++ b/solution.py
@@ -20,9 +20,7 @@
 
 PIECES = (("far", 0, 512), ("far", 512, 512), ("own", 0, 512), ("own", 512, 256), ("own", 768, 256))
 GROUPS = ((4, 3, -3), (2, -2), (1, -1, 0))
-ROUTES = tuple(
-    (dz, dx) for dz in (4, 3, -3, 2, -2, 1, -1, 0) for dx in (0, 1) if (dz, dx) != (0, 0)
-)
+ROUTES = ((4, 1), (3, 1), (-3, 1), (2, 1), (-2, 1), (1, 1), (-1, 1), (0, 1), (4, 0), (3, 0), (-3, 0), (2, 0), (-2, 0), (1, 0), (-1, 0))
 
 
 def split_two(x):
@@ -372,6 +370,23 @@
         all_rows(last, last + g, len(band)).wait_send()
     all_small(w_recv, w_sem).wait_send()
     all_small(s_recv, s_sem).wait_send()
+
+
+STORES = 6
+
+
+def store(update_ref, router_ref, update_hbm, router_hbm, sem):
+    copies = [pltpu.make_async_copy(router_ref, router_hbm, sem.at[STORES])]
+    step = update_ref.shape[0] // STORES
+    for i in range(STORES):
+        rows = pl.ds(i * step, step)
+        copies.append(
+            pltpu.make_async_copy(update_ref.at[rows, :], update_hbm.at[rows, :], sem.at[i])
+        )
+    for copy in copies:
+        copy.start()
+    for copy in copies:
+        copy.wait()
 
 
 def local(grad_out, router_weights, expert_ids, hidden, master, moment, second):
@@ -429,6 +444,17 @@
         expert_ids[0].T, router_weights[0].T, grad_out[0], hidden[0, 0], master[0, 0],
         moment[0, 0], second[0, 0],
     )
+    update, router = pl.pallas_call(
+        store,
+        out_shape=(
+            jax.ShapeDtypeStruct((hid_n, half), F32),
+            jax.ShapeDtypeStruct((top, toks_n), F32),
+        ),
+        in_specs=[hbm, hbm],
+        out_specs=(hbm, hbm),
+        scratch_shapes=[dma((STORES + 1,))],
+        compiler_params=pltpu.CompilerParams(vmem_limit_bytes=1 << 20),
+    )(update, router)
     return (update[None, None], router.T[None])
 
 

time: 114 us -> 112 us (0.982)
  local copies, waits for them, and re-layouts: 2.27 us -> 0 us
    unnamed x2 -> x0, local copies, waits for them, and re-layouts: 2.27 us -> none
    pallas_call x0 -> x1, Pallas kernels: none -> 1.72 us  [local(): pl.pallas_call(store, out_shape=(jax.ShapeDtypeStruct((hid_n, half), F32)...]
where the time goes in v4:
time: 112 us
  Pallas kernels  112 us (100%)
    pallas_call x1, Pallas kernels, local(): pl.pallas_call(kernel, out_shape=(pltpu.VMEM((hid_n, half), F32), pltpu.V...  110 us

profile of v4, /device:TPU:8, one launch (start us, length us, event | category | flops | bytes accessed | tf_op | source)
XLA Modules:
  0.0 112.2 jit_solution(7911498435064640411)
XLA Ops:
  0.6 109.8 %shard_map.86 = (f32[768,1024]{1,0:T(8,128)S(1)}, f32[8,512]{1,0:T(8,128)S(1)}) custom-call(s32[8,512]{1,0:T(8,128)} %bitcast.20, bf16[8,512]{1,0:T(8,128)(2,1)} %bitcast.21, bf16[512,2048]{1,0:T(8,128)(2,1)} %bitcast.16, bf16[768,1024]{1,0:T(8,128)(2,1)} %bitcast.17, f32[768,1024]{1,0:T(8,128)} %bitcast.15, bf16[768,1024]{1,0:T(8,128)(2,1)} %bitcast.18, ...), custom_call_target="tpu_custom_call" | custom-call | tf_op jit(solution)/shard_map/pallas_call | solution.py:401
  110.5 1.7 %shard_map.87 = (f32[768,1024]{1,0:T(8,128)}, f32[8,512]{1,0:T(8,128)}) custom-call(f32[768,1024]{1,0:T(8,128)S(1)} %get-tuple-element.6.update_ref, f32[8,512]{1,0:T(8,128)S(1)} %get-tuple-element.7.router_ref), custom_call_target="tpu_custom_call" | custom-call | tf_op jit(solution)/shard_map/pallas_call | solution.py:447

commit v5 on v4

--- a/solution.py
+++ b/solution.py
@@ -19,7 +19,7 @@
 BF16 = jnp.bfloat16
 
 PIECES = (("far", 0, 512), ("far", 512, 512), ("own", 0, 512), ("own", 512, 256), ("own", 768, 256))
-GROUPS = ((4, 3, -3), (2, -2), (1, -1, 0))
+GROUPS = ((6, 5), (4,), (3,), (2,), (1,))
 ROUTES = ((4, 1), (3, 1), (-3, 1), (2, 1), (-2, 1), (1, 1), (-1, 1), (0, 1), (4, 0), (3, 0), (-3, 0), (2, 0), (-2, 0), (1, 0), (-1, 0))
 
 
@@ -76,7 +76,8 @@
         (section, lax.rem(z + dz + 8, 8) * 2 + (lax.rem(xh + dx, 2))) for dz, dx in ROUTES
     ]
     bands = [
-        [peer for (dz, _), peer in zip(ROUTES, peers) if dz in group_dz] for group_dz in GROUPS
+        [peer for (dz, dx), peer in zip(ROUTES, peers) if abs(dz) + 2 * dx in hops]
+        for hops in GROUPS
     ]
     barrier = pltpu.get_barrier_semaphore()
     for peer in peers:
@@ -339,12 +340,13 @@
         line = contract_last(jnp.ones((8, 256), BF16), jnp.concatenate(split_two(total), 1))
         return jnp.concatenate([line, jnp.zeros((8, 128 - cap), F32)], 1)
 
-    s_recv[me] = score_of(me)
+
     for g, band in enumerate(bands):
         all_rows(last, last + g, len(band)).wait_recv()
         for peer in band:
             s_send[peer[1]] = score_of(peer[1])
             small_copy(s_send, s_recv, s_sem, peer[1], peer).start()
+    s_recv[me] = score_of(me)
     finish(last)
 
     all_small(s_recv, s_sem).wait_recv()

time: 112 us -> 112 us (level)
  no operation moved by 1% of the time
where the time goes in v5:
time: 112 us
  Pallas kernels  111 us (99%)
    pallas_call x1, Pallas kernels, local(): pl.pallas_call(kernel, out_shape=(pltpu.VMEM((hid_n, half), F32), pltpu.V...  109 us

profile of v5, /device:TPU:8, one launch (start us, length us, event | category | flops | bytes accessed | tf_op | source)
XLA Modules:
  0.0 111.6 jit_solution(5384024698237845234)
XLA Ops:
  0.6 109.2 %shard_map.86 = (f32[768,1024]{1,0:T(8,128)S(1)}, f32[8,512]{1,0:T(8,128)S(1)}) custom-call(s32[8,512]{1,0:T(8,128)} %bitcast.20, bf16[8,512]{1,0:T(8,128)(2,1)} %bitcast.21, bf16[512,2048]{1,0:T(8,128)(2,1)} %bitcast.16, bf16[768,1024]{1,0:T(8,128)(2,1)} %bitcast.17, f32[768,1024]{1,0:T(8,128)} %bitcast.15, bf16[768,1024]{1,0:T(8,128)(2,1)} %bitcast.18, ...), custom_call_target="tpu_custom_call" | custom-call | tf_op jit(solution)/shard_map/pallas_call | solution.py:403
  109.9 1.7 %shard_map.87 = (f32[768,1024]{1,0:T(8,128)}, f32[8,512]{1,0:T(8,128)}) custom-call(f32[768,1024]{1,0:T(8,128)S(1)} %get-tuple-element.6.update_ref, f32[8,512]{1,0:T(8,128)S(1)} %get-tuple-element.7.router_ref), custom_call_target="tpu_custom_call" | custom-call | tf_op jit(solution)/shard_map/pallas_call | solution.py:449

commit v6 on v5

--- a/solution.py
+++ b/solution.py
@@ -338,7 +338,7 @@
         for q in range(width // 128):
             total = total + product[:, q * 128 : (q + 1) * 128]
         line = contract_last(jnp.ones((8, 256), BF16), jnp.concatenate(split_two(total), 1))
-        return jnp.concatenate([line, jnp.zeros((8, 128 - cap), F32)], 1)
+        return jnp.concatenate([line, jnp.zeros((8, 128 - cap), F32)], 1)[0:1, :]
 
 
     for g, band in enumerate(bands):
@@ -428,8 +428,8 @@
             pltpu.VMEM((hid_n, 256), F32),
             pltpu.VMEM((16, 8, 128), F32),
             pltpu.VMEM((16, 8, 128), F32),
-            pltpu.VMEM((16, 8, 128), F32),
-            pltpu.VMEM((16, 8, 128), F32),
+            pltpu.VMEM((16, 1, 128), F32),
+            pltpu.VMEM((16, 1, 128), F32),
             dma((pieces,)),
             dma((4,)),
             dma((pieces + len(GROUPS) - 1,)),

time: 112 us -> 112 us (level)
  no operation moved by 1% of the time
where the time goes in v6:
time: 112 us; the launch traced here: 111 us
  Pallas kernels  111 us (99%)
    pallas_call x1, Pallas kernels, local(): pl.pallas_call(kernel, out_shape=(pltpu.VMEM((hid_n, half), F32), pltpu.V...  109 us

profile of v6, /device:TPU:8, one launch (start us, length us, event | category | flops | bytes accessed | tf_op | source)
XLA Modules:
  0.0 111.5 jit_solution(10063582578915025229)
XLA Ops:
  0.6 109.1 %shard_map.86 = (f32[768,1024]{1,0:T(8,128)S(1)}, f32[8,512]{1,0:T(8,128)S(1)}) custom-call(s32[8,512]{1,0:T(8,128)} %bitcast.20, bf16[8,512]{1,0:T(8,128)(2,1)} %bitcast.21, bf16[512,2048]{1,0:T(8,128)(2,1)} %bitcast.16, bf16[768,1024]{1,0:T(8,128)(2,1)} %bitcast.17, f32[768,1024]{1,0:T(8,128)} %bitcast.15, bf16[768,1024]{1,0:T(8,128)(2,1)} %bitcast.18, ...), custom_call_target="tpu_custom_call" | custom-call | tf_op jit(solution)/shard_map/pallas_call | solution.py:403
  109.7 1.7 %shard_map.87 = (f32[768,1024]{1,0:T(8,128)}, f32[8,512]{1,0:T(8,128)}) custom-call(f32[768,1024]{1,0:T(8,128)S(1)} %get-tuple-element.6.update_ref, f32[8,512]{1,0:T(8,128)S(1)} %get-tuple-element.7.router_ref), custom_call_target="tpu_custom_call" | custom-call | tf_op jit(solution)/shard_map/pallas_call | solution.py:449
